TPU v7x, 32 devices: a whole 2x2x4 slice. The times are simulated.
32 devices in a mesh: leaf: 8 (over y, x, core), rhs: 4 (over z).
Axes of the slice: x: 2, y: 2, z: 4, core: 2. Of those that a mesh axis runs over, the one named last changes fastest.
Arguments:
- coeffs: float32 [2, 64, 32, 128], P(None, 'rhs', 'leaf'), may hold values from -6 to 6
- own_factors: bfloat16 [6, 2, 32, 128, 128], P(None, None, 'leaf'), may hold values from -0.25 to 0.25
- cross_factors: bfloat16 [6, 2, 32, 128, 128], P(None, None, 'leaf'), may hold values from -0.25 to 0.25
- pattern: int32 [6, 32], P(None, 'leaf'), may hold values 0 or 1
- order: int32 [128], replicated, may hold values from 0 to 127, each once
Outputs:
- values: float32 [2, 64, 512, 8], P(None, 'rhs', 'leaf')
Inputs may be any that keep to these rules, and one draw needn't show every extreme that they name: order names each of 0 to 127 once.
All inputs are finite; a program needn't handle non-finite values. No bound on the sum of `pattern` on one device may be relied on, other than what follows from the above.
Results may differ from a plain program's by a relative error of at most 0.007.
Values may be sent and summed in bfloat16 or wider, within the bound.
A program may use at most 64 MiB of HBM per device.

v0:
```python
import jax
import jax.numpy as jnp
from jax import lax
from jax.sharding import PartitionSpec as P


def from_partner(block, axis, bit):
    count = lax.axis_size(axis)
    route = []
    for low in range(count):
        high = low | 1 << bit
        if high != low and high < count:
            route += [(low, high), (high, low)]
    return lax.ppermute(block, axis, route)


def contract(left_factor, right_factor):
    return jnp.einsum("heq,eqx->hex", left_factor, right_factor, preferred_element_type=jnp.float32)


def complex_apply(rounded, factors):
    real_part = contract(rounded[0], factors[0]) - contract(rounded[1], factors[1])
    imag_part = contract(rounded[0], factors[1]) + contract(rounded[1], factors[0])
    return jnp.stack([real_part, imag_part])


def apply_levels(state, own_factors, cross_factors, pattern, leaf_bits):
    for level in range(own_factors.shape[0]):
        pair_bit = leaf_bits - 1 - level % leaf_bits
        rounded = state.astype(jnp.bfloat16)
        self_term = complex_apply(rounded, own_factors[level])
        cross_term = complex_apply(rounded, cross_factors[level])
        incoming = from_partner(cross_term, "leaf", pair_bit)
        weight_matrix = pattern[level].astype(jnp.float32)[None, None, :, None]
        state = self_term + weight_matrix * incoming
    return state


def local(coeffs, own_factors, cross_factors, pattern, order):
    leaf_bits = lax.axis_size("leaf").bit_length() - 1
    local_blocks = coeffs.shape[2]
    state = apply_levels(coeffs, own_factors, cross_factors, pattern, leaf_bits)
    selected_rows = jnp.take(state, order, axis=3)
    flat = selected_rows.reshape(
        2, selected_rows.shape[1], local_blocks * selected_rows.shape[3], 1
    )
    return lax.all_to_all(flat, "leaf", split_axis=2, concat_axis=3, tiled=True)


def solution(mesh):
    in_specs = (
        P(None, "rhs", "leaf", None),
        P(None, None, "leaf", None, None),
        P(None, None, "leaf", None, None),
        P(None, "leaf"),
        P(),
    )
    out_specs = P(None, "rhs", "leaf", None)
    return jax.shard_map(local, mesh=mesh, in_specs=in_specs, out_specs=out_specs, check_vma=False)
```

profile of v0, /device:TPU:0, one launch (start us, length us, event | category | flops | bytes accessed | tf_op | source)
XLA Modules:
  0.0 49.6 jit_solution(18018178355052465947)
XLA Ops:
  0.0 1.0 %copy.16 = bf16[2,16,4,128]{3,1,2,0:T(8,128)(2,1)S(1)} copy(f32[2,16,4,128]{3,2,1,0:T(4,128)} %param.5) | data formatting | bytes 98304 | tf_op args[0]
  1.0 1.2 %fusion.85 = f32[4,128,16]{1,2,0:T(8,128)S(1)} fusion(bf16[6,2,4,128,128]{4,3,2,1,0:T(8,128)(2,1)} %param.7, bf16[2,16,4,128]{3,1,2,0:T(8,128)(2,1)S(1)} %copy.16), kind=kOutput, calls=%fused_computation.110 | convolution fusion | flops 2097152 | bytes 180224 | tf_op jit(solution)/shard_map/heq,eqx->hex/dot_general | solution.py:18
  2.2 1.1 %fusion.87 = f32[4,128,16]{1,2,0:T(8,128)S(1)} fusion(bf16[6,2,4,128,128]{4,3,2,1,0:T(8,128)(2,1)} %param.7, bf16[2,16,4,128]{3,1,2,0:T(8,128)(2,1)S(1)} %copy.16), kind=kOutput, calls=%fused_computation.112 | convolution fusion | flops 2097152 | bytes 180224 | tf_op jit(solution)/shard_map/heq,eqx->hex/dot_general | solution.py:18
  3.2 1.1 %fusion = f32[1,16,4,128]{3,1,2,0:T(8,128)S(1)} fusion(f32[4,128,16]{1,2,0:T(8,128)S(1)} %fusion.85, bf16[6,2,4,128,128]{4,3,2,1,0:T(8,128)(2,1)} %param.7, bf16[2,16,4,128]{3,1,2,0:T(8,128)(2,1)S(1)} %copy.16), kind=kOutput, calls=%fused_computation.2 | convolution fusion | flops 2105344 | bytes 212992 | tf_op jit(solution)/shard_map/heq,eqx->hex/dot_general | solution.py:18
  4.3 1.1 %fusion.1 = f32[1,16,4,128]{3,1,2,0:T(8,128)S(1)} fusion(f32[4,128,16]{1,2,0:T(8,128)S(1)} %fusion.87, bf16[6,2,4,128,128]{4,3,2,1,0:T(8,128)(2,1)} %param.7, bf16[2,16,4,128]{3,1,2,0:T(8,128)(2,1)S(1)} %copy.16), kind=kOutput, calls=%fused_computation.4 | convolution fusion | flops 2105344 | bytes 212992 | tf_op jit(solution)/shard_map/heq,eqx->hex/dot_general | solution.py:18
  5.3 3.1 %collective-permute-start = (f32[2,16,4,128]{3,1,2,0:T(8,128)S(1)}, f32[2,16,4,128]{3,1,2,0:T(8,128)S(1)}, u32[]{:S(2)}, u32[]{:S(2)}) collective-permute-start(f32[2,16,4,128]{3,1,2,0:T(8,128)S(1)} %pad_maximum_fusion), channel_id=1, source_target_pairs={{0,16},{16,0},{4,20},{20,4},{8,24},{24,8},{12,28},{28,12},{1,17},{... | collective-permute-start | bytes 196616 | tf_op jit(solution)/shard_map/ppermute | solution.py:14
  8.4 1.0 %fusion.93 = f32[4,128,16]{1,2,0:T(8,128)S(1)} fusion(bf16[6,2,4,128,128]{4,3,2,1,0:T(8,128)(2,1)} %param.6, bf16[2,16,4,128]{3,1,2,0:T(8,128)(2,1)S(1)} %copy.16), kind=kOutput, calls=%fused_computation.118 | convolution fusion | flops 2097152 | bytes 180224 | tf_op jit(solution)/shard_map/heq,eqx->hex/dot_general | solution.py:18
  9.4 1.1 %fusion.91 = f32[4,128,16]{1,2,0:T(8,128)S(1)} fusion(bf16[6,2,4,128,128]{4,3,2,1,0:T(8,128)(2,1)} %param.6, bf16[2,16,4,128]{3,1,2,0:T(8,128)(2,1)S(1)} %copy.16), kind=kOutput, calls=%fused_computation.116 | convolution fusion | flops 2097152 | bytes 180224 | tf_op jit(solution)/shard_map/heq,eqx->hex/dot_general | solution.py:18
  10.5 0.7 %compare_select_fusion = s32[128]{0:T(128)S(1)} fusion(s32[128]{0:T(128)} %param.9), kind=kLoop, calls=%fused_computation.201 | loop fusion | flops 384 | bytes 1024 | tf_op jit(solution)/shard_map/jit(_take)/jit(_where)/select_n | solution.py:43
  11.2 0.7 %compare_and_fusion = pred[128]{0:T(512)(128)(4,1)S(1)} fusion(s32[128]{0:T(128)} %param.9), kind=kLoop, calls=%fused_computation.208 | loop fusion | flops 768 | bytes 640 | tf_op jit(solution)/shard_map/jit(_take)/and | solution.py:43
  11.8 1.0 %fusion.3 = f32[1,16,4,128]{3,1,2,0:T(8,128)S(1)} fusion(f32[4,128,16]{1,2,0:T(8,128)S(1)} %fusion.93, bf16[6,2,4,128,128]{4,3,2,1,0:T(8,128)(2,1)} %param.6, bf16[2,16,4,128]{3,1,2,0:T(8,128)(2,1)S(1)} %copy.16), kind=kOutput, calls=%fused_computation.8 | convolution fusion | flops 2105344 | bytes 212992 | tf_op jit(solution)/shard_map/heq,eqx->hex/dot_general | solution.py:18
  12.9 1.1 %fusion.2 = f32[1,16,4,128]{3,1,2,0:T(8,128)S(1)} fusion(f32[4,128,16]{1,2,0:T(8,128)S(1)} %fusion.91, bf16[6,2,4,128,128]{4,3,2,1,0:T(8,128)(2,1)} %param.6, bf16[2,16,4,128]{3,1,2,0:T(8,128)(2,1)S(1)} %copy.16), kind=kOutput, calls=%fused_computation.6 | convolution fusion | flops 2105344 | bytes 212992 | tf_op jit(solution)/shard_map/heq,eqx->hex/dot_general | solution.py:18
  13.9 0.3 convert_reduce_fusion
  14.6 1.0 %fusion.82 = f32[4,16,128]{2,1,0:T(8,128)S(1)} fusion(bf16[6,2,4,128,128]{4,3,2,1,0:T(8,128)(2,1)} %param.6, bf16[2,16,4,128]{3,1,2,0:T(8,128)(2,1)S(1)} %fusion.144), kind=kOutput, calls=%fused_computation.107 | convolution fusion | flops 2097152 | bytes 180224 | tf_op jit(solution)/shard_map/heq,eqx->hex/dot_general | solution.py:18
  15.6 1.1 %fusion.78 = f32[4,16,128]{2,1,0:T(8,128)S(1)} fusion(bf16[6,2,4,128,128]{4,3,2,1,0:T(8,128)(2,1)} %param.6, bf16[2,16,4,128]{3,1,2,0:T(8,128)(2,1)S(1)} %fusion.144), kind=kOutput, calls=%fused_computation.103 | convolution fusion | flops 2097152 | bytes 180224 | tf_op jit(solution)/shard_map/heq,eqx->hex/dot_general | solution.py:18
  16.7 0.2 fusion.21
  16.9 0.2 fusion.20
  17.0 1.6 %collective-permute-start.1 = (f32[2,16,4,128]{3,1,2,0:T(8,128)S(1)}, f32[2,16,4,128]{3,1,2,0:T(8,128)S(1)}, u32[]{:S(2)}, u32[]{:S(2)}) collective-permute-start(f32[2,16,4,128]{3,1,2,0:T(8,128)S(1)} %pad_maximum_fusion.1), channel_id=1, source_target_pairs={{0,8},{8,0},{4,12},{12,4},{16,24},{24,16},{20,28},{28,20},{1,9},{9... | collective-permute-start | bytes 196616 | tf_op jit(solution)/shard_map/ppermute | solution.py:14
  18.7 0.2 fusion.22
  18.9 2.5 %collective-permute-done.1 = f32[2,16,4,128]{3,1,2,0:T(8,128)S(1)} collective-permute-done((f32[2,16,4,128]{3,1,2,0:T(8,128)S(1)}, f32[2,16,4,128]{3,1,2,0:T(8,128)S(1)}, u32[]{:S(2)}, u32[]{:S(2)}) %collective-permute-start.1) | collective-permute-done | bytes 65568 | tf_op jit(solution)/shard_map/ppermute | solution.py:14
  21.7 0.2 fusion.70
  22.0 0.2 fusion.17
  22.2 0.2 fusion.16
  22.6 0.2 fusion.18
  22.7 0.9 %collective-permute-done.2 = f32[2,16,4,128]{3,1,2,0:T(8,128)S(1)} collective-permute-done((f32[2,16,4,128]{3,1,2,0:T(8,128)S(1)}, f32[2,16,4,128]{3,1,2,0:T(8,128)S(1)}, u32[]{:S(2)}, u32[]{:S(2)}) %collective-permute-start.2) | collective-permute-done | bytes 65568 | tf_op jit(solution)/shard_map/ppermute | solution.py:14
  24.3 0.2 fusion.13
  24.5 0.2 fusion.12
  25.0 4.0 %collective-permute-done.3 = f32[2,16,4,128]{3,1,2,0:T(8,128)S(1)} collective-permute-done((f32[2,16,4,128]{3,1,2,0:T(8,128)S(1)}, f32[2,16,4,128]{3,1,2,0:T(8,128)S(1)}, u32[]{:S(2)}, u32[]{:S(2)}) %collective-permute-start.3) | collective-permute-done | bytes 65568 | tf_op jit(solution)/shard_map/ppermute | solution.py:14
  29.4 0.2 fusion.46
  29.7 0.2 fusion.9
  29.8 0.2 fusion.8
  30.0 1.6 %collective-permute-start.4 = (f32[2,16,4,128]{3,1,2,0:T(8,128)S(1)}, f32[2,16,4,128]{3,1,2,0:T(8,128)S(1)}, u32[]{:S(2)}, u32[]{:S(2)}) collective-permute-start(f32[2,16,4,128]{3,1,2,0:T(8,128)S(1)} %pad_maximum_fusion.4), channel_id=1, source_target_pairs={{0,8},{8,0},{4,12},{12,4},{16,24},{24,16},{20,28},{28,20},{1,9},{9... | collective-permute-start | bytes 196616 | tf_op jit(solution)/shard_map/ppermute | solution.py:14
  31.8 2.5 %collective-permute-done.4 = f32[2,16,4,128]{3,1,2,0:T(8,128)S(1)} collective-permute-done((f32[2,16,4,128]{3,1,2,0:T(8,128)S(1)}, f32[2,16,4,128]{3,1,2,0:T(8,128)S(1)}, u32[]{:S(2)}, u32[]{:S(2)}) %collective-permute-start.4) | collective-permute-done | bytes 65568 | tf_op jit(solution)/shard_map/ppermute | solution.py:14
  34.7 0.2 fusion.34
  35.0 0.2 fusion.5
  35.1 0.2 fusion.4
  35.5 0.2 fusion.6
  35.7 0.9 %collective-permute-done.5 = f32[2,16,4,128]{3,1,2,0:T(8,128)S(1)} collective-permute-done((f32[2,16,4,128]{3,1,2,0:T(8,128)S(1)}, f32[2,16,4,128]{3,1,2,0:T(8,128)S(1)}, u32[]{:S(2)}, u32[]{:S(2)}) %collective-permute-start.5) | collective-permute-done | bytes 65568 | tf_op jit(solution)/shard_map/ppermute | solution.py:14
  36.7 0.2 copy.11
  36.9 0.9 %gather_fusion = f32[128,2,16,4]{2,3,1,0:T(4,128)S(1)} fusion(f32[2,16,4,128]{1,2,3,0:T(4,128)S(1)} %copy.11, s32[1024]{0:T(1024)S(1)} %pad_clamp_fusion), kind=kCustom, calls=%fused_computation | custom fusion | bytes 131584 | tf_op jit(solution)/shard_map/jit(_take)/gather | solution.py:43
  37.9 0.2 copy.12
  38.2 0.2 copy.13
  38.4 0.7 %reshape.116 = f32[8,1,2048]{2,1,0:T(1,128)S(1)} reshape(f32[512,1,2,16]{3,2,1,0:T(2,128)S(1)} %bitcast.298) | data formatting | bytes 131072
  39.1 7.6 %all_to_all.18 = f32[8,1,2048]{2,1,0:T(1,128)S(1)} all-to-all(f32[8,1,2048]{2,1,0:T(1,128)S(1)} %reshape.116), channel_id=1, replica_groups=mesh['leaf'=8,'rhs'=4] {'leaf'}, dimensions={0} | all-to-all | bytes 131072 | tf_op jit(solution)/shard_map/all_to_all | solution.py:47
  46.7 0.5 %broadcast.28 = f32[]{:T(128)} broadcast(f32[]{:T(128)} %constant.140), dimensions={} | broadcast | bytes 8 | tf_op jit(solution)/shard_map/all_to_all | solution.py:47
  47.2 0.8 %reduce.12 = f32[8,2048]{1,0:T(8,128)S(1)} reduce(f32[8,1,2048]{2,1,0:T(1,128)S(1)} %all_to_all.18, f32[]{:T(128)} %broadcast.28), dimensions={1}, to_apply=%all_to_all.13.reduce_sub_computation | reduce | bytes 131076 | tf_op jit(solution)/shard_map/all_to_all | solution.py:47
  48.0 0.7 %reshape.117 = f32[512,1,2,16]{3,2,1,0:T(2,128)S(1)} reshape(f32[8,2048]{1,0:T(8,128)S(1)} %reduce.12) | data formatting | bytes 131072
  48.7 0.9 %copy.14 = f32[2,16,8,64,1]{3,2,1,0,4:T(8,128)} copy(f32[2,16,8,64,1]{1,0,3,2,4:T(2,128)S(1)} %bitcast.297) | data formatting | bytes 131072 | tf_op jit(solution)/shard_map/all_to_all | solution.py:47
  (48 shorter events, 4.1 us)
Async XLA Ops:
  0.0 14.3 %copy-start = (bf16[6,2,4,128,128]{4,3,2,1,0:T(8,128)(2,1)S(1)}, bf16[6,2,4,128,128]{4,3,2,1,0:T(8,128)(2,1)}, u32[]{:S(2)}) copy-start(bf16[6,2,4,128,128]{4,3,2,1,0:T(8,128)(2,1)} %param.7) | copy-start | bytes 4718596
  0.0 13.9 %copy-start.2 = (s32[6,4]{0,1:T(4,128)S(1)}, s32[6,4]{0,1:T(4,128)}, u32[]{:S(2)}) copy-start(s32[6,4]{0,1:T(4,128)} %param.8) | copy-start | bytes 292
  1.0 17.6 %copy-start.1 = (bf16[6,2,4,128,128]{4,3,2,1,0:T(8,128)(2,1)S(1)}, bf16[6,2,4,128,128]{4,3,2,1,0:T(8,128)(2,1)}, u32[]{:S(2)}) copy-start(bf16[6,2,4,128,128]{4,3,2,1,0:T(8,128)(2,1)} %param.6) | copy-start | bytes 4718596
  5.3 8.9 %collective-permute-start = (f32[2,16,4,128]{3,1,2,0:T(8,128)S(1)}, f32[2,16,4,128]{3,1,2,0:T(8,128)S(1)}, u32[]{:S(2)}, u32[]{:S(2)}) collective-permute-start(f32[2,16,4,128]{3,1,2,0:T(8,128)S(1)} %pad_maximum_fusion), channel_id=1, source_target_pairs={{0,16},{16,0},{4,20},{20,4},{8,24},{24,8},{12,28},{28,12},{1,17},{... | collective-permute-start | bytes 196616 | tf_op jit(solution)/shard_map/ppermute | solution.py:14
  17.0 4.3 %collective-permute-start.1 = (f32[2,16,4,128]{3,1,2,0:T(8,128)S(1)}, f32[2,16,4,128]{3,1,2,0:T(8,128)S(1)}, u32[]{:S(2)}, u32[]{:S(2)}) collective-permute-start(f32[2,16,4,128]{3,1,2,0:T(8,128)S(1)} %pad_maximum_fusion.1), channel_id=1, source_target_pairs={{0,8},{8,0},{4,12},{12,4},{16,24},{24,16},{20,28},{28,20},{1,9},{9... | collective-permute-start | bytes 196616 | tf_op jit(solution)/shard_map/ppermute | solution.py:14
  22.3 1.3 %collective-permute-start.2 = (f32[2,16,4,128]{3,1,2,0:T(8,128)S(1)}, f32[2,16,4,128]{3,1,2,0:T(8,128)S(1)}, u32[]{:S(2)}, u32[]{:S(2)}) collective-permute-start(f32[2,16,4,128]{3,1,2,0:T(8,128)S(1)} %pad_maximum_fusion.2), channel_id=1, source_target_pairs={{0,4},{4,0},{8,12},{12,8},{16,20},{20,16},{24,28},{28,24},{1,5},{5... | collective-permute-start | bytes 196616 | tf_op jit(solution)/shard_map/ppermute | solution.py:14
  24.7 4.3 %collective-permute-start.3 = (f32[2,16,4,128]{3,1,2,0:T(8,128)S(1)}, f32[2,16,4,128]{3,1,2,0:T(8,128)S(1)}, u32[]{:S(2)}, u32[]{:S(2)}) collective-permute-start(f32[2,16,4,128]{3,1,2,0:T(8,128)S(1)} %pad_maximum_fusion.3), channel_id=1, source_target_pairs={{0,16},{16,0},{4,20},{20,4},{8,24},{24,8},{12,28},{28,12},{1,17},{... | collective-permute-start | bytes 196616 | tf_op jit(solution)/shard_map/ppermute | solution.py:14
  30.0 4.3 %collective-permute-start.4 = (f32[2,16,4,128]{3,1,2,0:T(8,128)S(1)}, f32[2,16,4,128]{3,1,2,0:T(8,128)S(1)}, u32[]{:S(2)}, u32[]{:S(2)}) collective-permute-start(f32[2,16,4,128]{3,1,2,0:T(8,128)S(1)} %pad_maximum_fusion.4), channel_id=1, source_target_pairs={{0,8},{8,0},{4,12},{12,4},{16,24},{24,16},{20,28},{28,20},{1,9},{9... | collective-permute-start | bytes 196616 | tf_op jit(solution)/shard_map/ppermute | solution.py:14
  35.3 1.3 %collective-permute-start.5 = (f32[2,16,4,128]{3,1,2,0:T(8,128)S(1)}, f32[2,16,4,128]{3,1,2,0:T(8,128)S(1)}, u32[]{:S(2)}, u32[]{:S(2)}) collective-permute-start(f32[2,16,4,128]{3,1,2,0:T(8,128)S(1)} %pad_maximum_fusion.5), channel_id=1, source_target_pairs={{0,4},{4,0},{8,12},{12,8},{16,20},{20,16},{24,28},{28,24},{1,5},{5... | collective-permute-start | bytes 196616 | tf_op jit(solution)/shard_map/ppermute | solution.py:14
where the time goes:
time: 50 us; the launch traced here: 49.6 us
  matrix products  16.3 us (33%)
  waiting for transfers between devices  10.8 us (22%)
  blocking collectives  7.58 us (15%)
  starting transfers between devices  6.4 us (13%)
  local copies, waits for them, and re-layouts  5.46 us (11%)
  other arithmetic  2.92 us (6%)
    dot_general x48, matrix products, contract(): jnp.einsum('heq,eqx->hex', left_factor, right_factor, preferred_element_t...  16.3 us
    ppermute x6, waiting for transfers between devices, from_partner(): return lax.ppermute(block, axis, route)  10.8 us
    all_to_all x1, blocking collectives, local(): return lax.all_to_all(flat, 'leaf', split_axis=2, concat_axis=3, tiled=True)  7.58 us
    ppermute x6, starting transfers between devices, from_partner(): return lax.ppermute(block, axis, route)  6.4 us
    unnamed x9, local copies, waits for them, and re-layouts  2.41 us
    all_to_all x2, local copies, waits for them, and re-layouts, local(): return lax.all_to_all(flat, 'leaf', split_axis=2, concat_axis=3, tiled=True)  1.36 us
    gather x3, local copies, waits for them, and re-layouts, local(): selected_rows = jnp.take(state, order, axis=3)  1.22 us
  transfers between devices with their start and end apart: 6, of which 5 were waited for; matrix products, arithmetic and copies ran while one was open for 15% of the time, Pallas kernels for 0%

commit v1 on v0

--- a/solution.py
+++ b/solution.py
@@ -1,7 +1,205 @@
+import functools
+
 import jax
 import jax.numpy as jnp
 from jax import lax
+from jax.experimental import pallas as pl
+from jax.experimental.pallas import tpu as pltpu
 from jax.sharding import PartitionSpec as P
+
+MESH = pl.DeviceIdType.MESH
+
+
+def flip(index, bit):
+    step = 1 << bit
+    return index + step - 2 * step * ((index // step) % 2)
+
+
+def stacked(state):
+    half = state.shape[0] // 2
+    rounded = state.astype(jnp.bfloat16)
+    real, imag = rounded[:half], rounded[half:]
+    turned = jnp.concatenate([-imag, real], axis=0)
+    return jnp.concatenate([rounded, turned], axis=1)
+
+
+def product(left, right):
+    return jnp.dot(left, right, preferred_element_type=jnp.float32)
+
+
+def window_kernel(
+    n, levels, blocks,
+    coeffs_hbm, own_hbm, cross_hbm, pattern_ref, order_ref, out_ref,
+    coeffs, own, cross, out_box, in_box, folded, mask_out, mask_in, last_out, last_in,
+    load_sem, own_sem, cross_sem, send_sem, recv_sem, mask_sem, last_send, last_recv,
+):
+    me = lax.axis_index("leaf")
+    bits = n.bit_length() - 1
+    pair_bit = [bits - 1 - level % bits for level in range(levels)]
+    last = levels - 1
+    rank = own.shape[-1]
+    rows = coeffs.shape[0] // blocks
+    parts = n // blocks
+    chunk = rank // parts
+
+    coeffs_copy = pltpu.make_async_copy(coeffs_hbm, coeffs, load_sem)
+    coeffs_copy.start()
+    own_copy, cross_copy = [], []
+    for level in range(levels):
+        cross_copy.append(pltpu.make_async_copy(cross_hbm.at[level], cross.at[level], cross_sem.at[level]))
+        own_copy.append(pltpu.make_async_copy(own_hbm.at[level], own.at[level], own_sem.at[level]))
+        cross_copy[level].start()
+        own_copy[level].start()
+
+    barrier = pltpu.get_barrier_semaphore()
+    for delta in range(1, n):
+        pl.semaphore_signal(barrier, inc=1, device_id={"leaf": lax.rem(me + delta, n)}, device_id_type=MESH)
+
+    masks = pattern_ref[...].astype(jnp.float32)
+    for block in range(blocks):
+        mask_out[block : block + 1, :] = jnp.broadcast_to(masks[block : block + 1, last : last + 1], (1, rank))
+
+    def mask_of(level, block):
+        return jnp.broadcast_to(masks[block : block + 1, level : level + 1], (1, rank))
+
+    def factor(ref, level, block):
+        return ref[level, :, block].reshape(2 * rank, rank)
+
+    def exchange(level, block):
+        return pltpu.make_async_remote_copy(
+            src_ref=out_box.at[level, block],
+            dst_ref=in_box.at[level, block],
+            send_sem=send_sem.at[level, block],
+            recv_sem=recv_sem.at[level, block],
+            device_id={"leaf": flip(me, pair_bit[level])},
+            device_id_type=MESH,
+        )
+
+    order_row = jnp.broadcast_to(order_ref[...], (8, rank))
+    turned_row = pltpu.roll(order_row, chunk, 1)[0:1]
+    order_row = order_row[0:1]
+    source = lax.broadcasted_iota(jnp.int32, (rank, rank), 0)
+    low = lax.broadcasted_iota(jnp.int32, (rank, rank), 1) < chunk
+    straight = jnp.where(source == order_row, 1.0, 0.0)
+    shifted = jnp.where(source == turned_row, 1.0, 0.0)
+    pick_own = jnp.concatenate([jnp.where(low, straight, 0.0), jnp.where(low, shifted, 0.0)], axis=1).astype(jnp.bfloat16)
+    pick_cross = jnp.concatenate([jnp.where(low, 0.0, shifted), jnp.where(low, 0.0, straight)], axis=1)
+
+    def fold(block):
+        mask = mask_in[block : block + 1, :]
+        mask = jnp.concatenate([mask, mask], axis=1)
+        pick = jnp.concatenate([pick_own, (pick_cross * mask).astype(jnp.bfloat16)], axis=0)
+        both = jnp.concatenate([factor(own, last, block), factor(cross, last, block)], axis=1)
+        folded[block] = product(both, pick).astype(jnp.bfloat16)
+
+    mask_copy = pltpu.make_async_remote_copy(
+        src_ref=mask_out, dst_ref=mask_in, send_sem=mask_sem.at[0], recv_sem=mask_sem.at[1],
+        device_id={"leaf": flip(me, pair_bit[last])}, device_id_type=MESH,
+    )
+
+    kept = [None] * blocks
+    coeffs_copy.wait()
+    for level in range(last):
+        cross_copy[level].wait()
+        mask = [mask_of(level - 1, block) for block in range(blocks)] if level else None
+        for block in range(blocks):
+            if level == 0:
+                state = coeffs[pl.ds(block, rows, stride=blocks), :]
+            else:
+                exchange(level - 1, block).wait_recv()
+                state = kept[block] + mask[block] * in_box[level - 1, block].astype(jnp.float32)
+            left = stacked(state)
+            out_box[level, block] = product(left, factor(cross, level, block)).astype(jnp.bfloat16)
+            if level == 0 and block == 0:
+                pl.semaphore_wait(barrier, n - 1)
+                mask_copy.start()
+            exchange(level, block).start()
+            if block == 0:
+                own_copy[level].wait()
+            kept[block] = product(left, factor(own, level, block))
+        if level == 1:
+            mask_copy.wait()
+            cross_copy[last].wait()
+            own_copy[last].wait()
+        if level in (1, 3):
+            for block in range(blocks):
+                if (block < blocks // 2) == (level == 1):
+                    fold(block)
+
+    mask = [mask_of(last - 1, block) for block in range(blocks)]
+    for block in range(blocks):
+        exchange(last - 1, block).wait_recv()
+        state = kept[block] + mask[block] * in_box[last - 1, block].astype(jnp.float32)
+        result = product(stacked(state), folded[block]).astype(jnp.bfloat16)
+        for part in range(parts):
+            target = block * parts + part
+            last_out[target] = result[:, part * rank : (part + 1) * rank]
+
+            @pl.when(target != me)
+            def _():
+                pltpu.make_async_remote_copy(
+                    src_ref=last_out.at[target], dst_ref=last_in.at[me],
+                    send_sem=last_send.at[target], recv_sem=last_recv.at[me],
+                    device_id={"leaf": target}, device_id_type=MESH,
+                ).start()
+
+            @pl.when(target == me)
+            def _():
+                last_in[me] = result[:, part * rank : (part + 1) * rank]
+
+    for level in range(last):
+        for block in range(blocks):
+            exchange(level, block).wait_send()
+
+    def final(peer):
+        return pltpu.make_async_remote_copy(
+            src_ref=last_out.at[peer], dst_ref=last_in.at[peer],
+            send_sem=last_send.at[peer], recv_sem=last_recv.at[peer],
+            device_id={"leaf": peer}, device_id_type=MESH,
+        )
+
+    for delta in range(1, n):
+        final(lax.rem(me + delta, n)).wait_recv()
+    for device in range(n):
+        mine = last_in[device].astype(jnp.float32)
+        other = last_in[device ^ (1 << pair_bit[last])].astype(jnp.float32)
+        value = mine + pltpu.roll(other, rank - chunk, 1)
+        out_ref[pl.ds(device, rows, stride=n), :] = value[:, :chunk]
+    for delta in range(1, n):
+        final(lax.rem(me + delta, n)).wait_send()
+
+
+def fused(coeffs, own_factors, cross_factors, pattern, order):
+    n = lax.axis_size("leaf")
+    pair, rhs, blocks, rank = coeffs.shape
+    levels = own_factors.shape[0]
+    rows = pair * rhs
+    chunk = rank * blocks // n
+    dma, bf16 = pltpu.SemaphoreType.DMA, jnp.bfloat16
+    anywhere, vmem = pl.BlockSpec(memory_space=pl.ANY), pl.BlockSpec(memory_space=pltpu.VMEM)
+    out = pl.pallas_call(
+        functools.partial(window_kernel, n, levels, blocks),
+        out_shape=jax.ShapeDtypeStruct((rows * n, chunk), jnp.float32),
+        in_specs=[anywhere, anywhere, anywhere, vmem, vmem],
+        out_specs=vmem,
+        scratch_shapes=[
+            pltpu.VMEM((rows * blocks, rank), jnp.float32),
+            pltpu.VMEM(own_factors.shape, bf16),
+            pltpu.VMEM(cross_factors.shape, bf16),
+            pltpu.VMEM((levels - 1, blocks, rows, rank), bf16),
+            pltpu.VMEM((levels - 1, blocks, rows, rank), bf16),
+            pltpu.VMEM((blocks, 2 * rank, 2 * rank), bf16),
+            pltpu.VMEM((max(blocks, 8), rank), jnp.float32),
+            pltpu.VMEM((max(blocks, 8), rank), jnp.float32),
+            pltpu.VMEM((n, rows, rank), bf16),
+            pltpu.VMEM((n, rows, rank), bf16),
+            dma, dma((levels,)), dma((levels,)),
+            dma((levels - 1, blocks)), dma((levels - 1, blocks)),
+            dma((2,)), dma((n,)), dma((n,)),
+        ],
+        compiler_params=pltpu.CompilerParams(collective_id=0, has_side_effects=True),
+    )(coeffs.reshape(rows * blocks, rank), own_factors, cross_factors, pattern.T, order.reshape(1, rank))
+    return jnp.transpose(out.reshape(pair, rhs, n, chunk), (0, 1, 3, 2))
 
 
 def from_partner(block, axis, bit):
@@ -36,15 +234,20 @@
     return state
 
 
-def local(coeffs, own_factors, cross_factors, pattern, order):
+def general(coeffs, own_factors, cross_factors, pattern, order):
     leaf_bits = lax.axis_size("leaf").bit_length() - 1
     local_blocks = coeffs.shape[2]
     state = apply_levels(coeffs, own_factors, cross_factors, pattern, leaf_bits)
     selected_rows = jnp.take(state, order, axis=3)
-    flat = selected_rows.reshape(
-        2, selected_rows.shape[1], local_blocks * selected_rows.shape[3], 1
-    )
+    flat = selected_rows.reshape(2, selected_rows.shape[1], local_blocks * selected_rows.shape[3], 1)
     return lax.all_to_all(flat, "leaf", split_axis=2, concat_axis=3, tiled=True)
+
+
+def local(coeffs, own_factors, cross_factors, pattern, order):
+    n, blocks = lax.axis_size("leaf"), coeffs.shape[2]
+    if n == 2 * blocks and n <= 8 and own_factors.shape[0] == 6:
+        return fused(coeffs, own_factors, cross_factors, pattern, order)
+    return general(coeffs, own_factors, cross_factors, pattern, order)
 
 
 def solution(mesh):

time: 50 us -> 23.8 us (0.48)
  Pallas kernels: 0 us -> 22.1 us
  matrix products: 16.3 us -> 0 us
  waiting for transfers between devices: 10.8 us -> 0 us
  blocking collectives: 7.58 us -> 0 us
  starting transfers between devices: 6.4 us -> 0 us
  local copies, waits for them, and re-layouts: 5.46 us -> 1.57 us
  other arithmetic: 2.92 us -> 0 us
    pallas_call x0 -> x1, Pallas kernels: none -> 22.1 us  [fused(): pl.pallas_call(functools.partial(window_kernel, n, levels, blocks), out_s...]
    dot_general x48 -> x0, matrix products: 16.3 us -> none  [contract(): jnp.einsum('heq,eqx->hex', left_factor, right_factor, preferred_element_t...]
    ppermute x6 -> x0, waiting for transfers between devices: 10.8 us -> none  [from_partner(): return lax.ppermute(block, axis, route)]
    all_to_all x1 -> x0, blocking collectives: 7.58 us -> none  [local(): return lax.all_to_all(flat, 'leaf', split_axis=2, concat_axis=3, tiled=True)]
    ppermute x6 -> x0, starting transfers between devices: 6.4 us -> none  [from_partner(): return lax.ppermute(block, axis, route)]
    all_to_all x2 -> x0, local copies, waits for them, and re-layouts: 1.36 us -> none  [local(): return lax.all_to_all(flat, 'leaf', split_axis=2, concat_axis=3, tiled=True)]
    gather x3 -> x0, local copies, waits for them, and re-layouts: 1.22 us -> none  [local(): selected_rows = jnp.take(state, order, axis=3)]
    unnamed x9 -> x1, local copies, waits for them, and re-layouts: 2.41 us -> 1.57 us
  transfers between devices with their start and end apart: 6 -> 0, of which waited for: 5 -> 0; matrix products, arithmetic and copies ran while one was open for 15% -> 0% of each run, Pallas kernels for 0% -> 0%
where the time goes in v1:
time: 23.8 us; the launch traced here: 23.6 us
  Pallas kernels  22.1 us (93%)
  local copies, waits for them, and re-layouts  1.57 us (7%)
    pallas_call x1, Pallas kernels, fused(): pl.pallas_call(functools.partial(window_kernel, n, levels, blocks), out_s...  22.1 us
    unnamed x1, local copies, waits for them, and re-layouts  1.57 us

profile of v1, /device:TPU:0, one launch (start us, length us, event | category | flops | bytes accessed | tf_op | source)
XLA Modules:
  0.0 23.6 jit_solution(16226011173353772818)
XLA Ops:
  0.0 22.1 %shard_map.55 = f32[256,64]{1,0:T(8,128)} custom-call(f32[128,128]{1,0:T(8,128)} %bitcast.7, bf16[6,2,4,128,128]{4,3,2,1,0:T(8,128)(2,1)} %own_hbm.1, bf16[6,2,4,128,128]{4,3,2,1,0:T(8,128)(2,1)} %cross_hbm.1, s32[4,6]{1,0:T(4,128)} %bitcast.8, s32[1,128]{1,0:T(1,128)} %bitcast.9), custom_call_target="tpu_custom_call" | custom-call | tf_op jit(solution)/shard_map/pallas_call | solution.py:180
  22.1 1.6 %copy.7 = f32[2,16,64,8]{2,3,1,0:T(8,128)} copy(f32[2,16,64,8]{2,3,1,0:T(8,128)} %bitcast.6) | data formatting | bytes 131072

commit v2 on v1

v2 whole, which is shorter than its diff:
```python
import functools

import jax
import jax.numpy as jnp
from jax import lax
from jax.experimental import pallas as pl
from jax.experimental.pallas import tpu as pltpu
from jax.sharding import PartitionSpec as P

MESH = pl.DeviceIdType.MESH
GROUPS = 2


def flip(index, bit):
    step = 1 << bit
    return index + step - 2 * step * ((index // step) % 2)


def stacked(state):
    half = state.shape[0] // 2
    rounded = state.astype(jnp.bfloat16)
    real, imag = rounded[:half], rounded[half:]
    turned = jnp.concatenate([-imag, real], axis=0)
    return jnp.concatenate([rounded, turned], axis=1)


def product(left, right):
    return jnp.dot(left, right, preferred_element_type=jnp.float32)


def window_kernel(
    n, levels, blocks, groups,
    coeffs_hbm, own_hbm, cross_hbm, pattern_hbm, order_hbm, last_in,
    coeffs, own, cross, pattern, order, out_box, in_box, folded, mask_out, mask_in, last_out,
    load_sem, own_sem, cross_sem, send_sem, recv_sem, mask_sem, last_send, last_recv,
):
    me = lax.axis_index("leaf")
    bits = n.bit_length() - 1
    pair_bit = [bits - 1 - level % bits for level in range(levels)]
    last = levels - 1
    rank = own.shape[-1]
    rows = coeffs.shape[0] // blocks
    parts = n // blocks
    chunk = rank // parts
    size = blocks // groups

    barrier = pltpu.get_barrier_semaphore()
    for delta in range(1, n):
        pl.semaphore_signal(barrier, inc=1, device_id={"leaf": lax.rem(me + delta, n)}, device_id_type=MESH)

    coeffs_copy = pltpu.make_async_copy(coeffs_hbm, coeffs, load_sem.at[0])
    pattern_copy = pltpu.make_async_copy(pattern_hbm, pattern, load_sem.at[1])
    order_copy = pltpu.make_async_copy(order_hbm, order, load_sem.at[2])
    own_copy = [pltpu.make_async_copy(own_hbm.at[k], own.at[k], own_sem.at[k]) for k in range(levels)]
    cross_copy = [pltpu.make_async_copy(cross_hbm.at[k], cross.at[k], cross_sem.at[k]) for k in range(levels)]
    coeffs_copy.start()
    cross_copy[0].start()
    pattern_copy.start()
    order_copy.start()
    own_copy[0].start()

    def exchange(level, group):
        span = pl.ds(group * size, size)
        return pltpu.make_async_remote_copy(
            src_ref=out_box.at[level, span],
            dst_ref=in_box.at[level, span],
            send_sem=send_sem.at[level, group],
            recv_sem=recv_sem.at[level, group],
            device_id={"leaf": flip(me, pair_bit[level])},
            device_id_type=MESH,
        )

    def factor(ref, level, block):
        return ref[level, :, block].reshape(2 * rank, rank)

    def mask_of(level, block):
        masks = pattern[...].astype(jnp.float32)
        return jnp.broadcast_to(masks[block : block + 1, level : level + 1], (1, rank))

    def picks():
        order_row = jnp.broadcast_to(order[...], (8, rank))
        turned_row = pltpu.roll(order_row, chunk, 1)[0:1]
        order_row = order_row[0:1]
        source = lax.broadcasted_iota(jnp.int32, (rank, rank), 0)
        low = lax.broadcasted_iota(jnp.int32, (rank, rank), 1) < chunk
        straight = jnp.where(source == order_row, 1.0, 0.0)
        shifted = jnp.where(source == turned_row, 1.0, 0.0)
        pick_own = jnp.concatenate([jnp.where(low, straight, 0.0), jnp.where(low, shifted, 0.0)], axis=1)
        pick_cross = jnp.concatenate([jnp.where(low, 0.0, shifted), jnp.where(low, 0.0, straight)], axis=1)
        return pick_own.astype(jnp.bfloat16), pick_cross

    def fold(block):
        pick_own, pick_cross = picks()
        mask = mask_in[block : block + 1, :]
        mask = jnp.concatenate([mask, mask], axis=1)
        pick = jnp.concatenate([pick_own, (pick_cross * mask).astype(jnp.bfloat16)], axis=0)
        both = jnp.concatenate([factor(own, last, block), factor(cross, last, block)], axis=1)
        folded[block] = product(both, pick).astype(jnp.bfloat16)

    mask_copy = pltpu.make_async_remote_copy(
        src_ref=mask_out, dst_ref=mask_in, send_sem=mask_sem.at[0], recv_sem=mask_sem.at[1],
        device_id={"leaf": flip(me, pair_bit[last])}, device_id_type=MESH,
    )

    kept = [None] * blocks
    left = [None] * blocks

    def states(level, group, mask):
        found = []
        for block in range(group * size, (group + 1) * size):
            if level == 0:
                found.append(coeffs[pl.ds(block, rows, stride=blocks), :])
            else:
                found.append(kept[block] + mask[block] * in_box[level - 1, block].astype(jnp.float32))
        return found

    coeffs_copy.wait()
    cross_copy[0].wait()
    for level in range(last):
        mask = [mask_of(level - 1, block) for block in range(blocks)] if level else None
        for group in range(groups):
            if level:
                exchange(level - 1, group).wait_recv()
            for index, state in enumerate(states(level, group, mask)):
                block = group * size + index
                left[block] = stacked(state)
                out_box[level, block] = product(left[block], factor(cross, level, block)).astype(jnp.bfloat16)
            if level == 0 and group == 0:
                pl.semaphore_wait(barrier, n - 1)
            exchange(level, group).start()
        if level == 0:
            for later in range(1, levels):
                cross_copy[later].start()
                own_copy[later].start()
            pattern_copy.wait()
            order_copy.wait()
            for block in range(blocks):
                mask_out[block : block + 1, :] = mask_of(last, block)
            mask_copy.start()
        own_copy[level].wait()
        for block in range(blocks):
            kept[block] = product(left[block], factor(own, level, block))
        if level == 1:
            mask_copy.wait()
            cross_copy[last].wait()
            own_copy[last].wait()
        if level in (1, 3):
            for block in range(blocks):
                if (block < blocks // 2) == (level == 1):
                    fold(block)
        if level < last - 1:
            cross_copy[level + 1].wait()

    mask = [mask_of(last - 1, block) for block in range(blocks)]
    for group in range(groups):
        exchange(last - 1, group).wait_recv()
        for index, state in enumerate(states(last, group, mask)):
            block = group * size + index
            result = product(stacked(state), folded[block]).astype(jnp.bfloat16)
            for part in range(parts):
                last_out[block * parts + part] = result[:, part * rank : (part + 1) * rank]
        for target in range(group * size * parts, (group + 1) * size * parts):

            @pl.when(target != me)
            def _():
                pltpu.make_async_remote_copy(
                    src_ref=last_out.at[target], dst_ref=last_in.at[me],
                    send_sem=last_send.at[target], recv_sem=last_recv.at[me],
                    device_id={"leaf": target}, device_id_type=MESH,
                ).start()

    last_in[me] = last_out[me]
    for level in range(last):
        for group in range(groups):
            exchange(level, group).wait_send()

    def final(peer):
        return pltpu.make_async_remote_copy(
            src_ref=last_out.at[peer], dst_ref=last_in.at[peer],
            send_sem=last_send.at[peer], recv_sem=last_recv.at[peer],
            device_id={"leaf": peer}, device_id_type=MESH,
        )

    for delta in range(1, n):
        final(lax.rem(me + delta, n)).wait_recv()
    for delta in range(1, n):
        final(lax.rem(me + delta, n)).wait_send()


def assemble_kernel(n, pair_bit, parts_ref, out_ref):
    rank = parts_ref.shape[2]
    rows, chunk = parts_ref.shape[1], out_ref.shape[1]
    for device in range(n):
        mine = parts_ref[device].astype(jnp.float32)
        other = parts_ref[device ^ (1 << pair_bit)].astype(jnp.float32)
        value = mine + pltpu.roll(other, rank - chunk, 1)
        out_ref[pl.ds(device, rows, stride=n), :] = value[:, :chunk]


def fused(coeffs, own_factors, cross_factors, pattern, order):
    n = lax.axis_size("leaf")
    pair, rhs, blocks, rank = coeffs.shape
    levels = own_factors.shape[0]
    rows = pair * rhs
    chunk = rank * blocks // n
    dma, bf16 = pltpu.SemaphoreType.DMA, jnp.bfloat16
    anywhere, vmem = pl.BlockSpec(memory_space=pl.ANY), pl.BlockSpec(memory_space=pltpu.VMEM)
    landed = pl.pallas_call(
        functools.partial(window_kernel, n, levels, blocks, GROUPS),
        out_shape=pltpu.VMEM((n, rows, rank), bf16),
        in_specs=[anywhere] * 5,
        out_specs=vmem,
        scratch_shapes=[
            pltpu.VMEM((rows * blocks, rank), jnp.float32),
            pltpu.VMEM(own_factors.shape, bf16),
            pltpu.VMEM(cross_factors.shape, bf16),
            pltpu.VMEM((blocks, levels), jnp.int32),
            pltpu.VMEM((1, rank), jnp.int32),
            pltpu.VMEM((levels - 1, blocks, rows, rank), bf16),
            pltpu.VMEM((levels - 1, blocks, rows, rank), bf16),
            pltpu.VMEM((blocks, 2 * rank, 2 * rank), bf16),
            pltpu.VMEM((max(blocks, 8), rank), jnp.float32),
            pltpu.VMEM((max(blocks, 8), rank), jnp.float32),
            pltpu.VMEM((n, rows, rank), bf16),
            dma((3,)), dma((levels,)), dma((levels,)),
            dma((levels - 1, GROUPS)), dma((levels - 1, GROUPS)),
            dma((2,)), dma((n,)), dma((n,)),
        ],
        compiler_params=pltpu.CompilerParams(collective_id=0, has_side_effects=True),
    )(coeffs.reshape(rows * blocks, rank), own_factors, cross_factors, pattern.T, order.reshape(1, rank))
    bits = n.bit_length() - 1
    out = pl.pallas_call(
        functools.partial(assemble_kernel, n, bits - 1 - (levels - 1) % bits),
        out_shape=jax.ShapeDtypeStruct((rows * n, chunk), jnp.float32),
        in_specs=[vmem],
        out_specs=vmem,
    )(pltpu.with_memory_space_constraint(landed, pltpu.VMEM))
    return jnp.transpose(out.reshape(pair, rhs, n, chunk), (0, 1, 3, 2))


def from_partner(block, axis, bit):
    count = lax.axis_size(axis)
    route = []
    for low in range(count):
        high = low | 1 << bit
        if high != low and high < count:
            route += [(low, high), (high, low)]
    return lax.ppermute(block, axis, route)


def contract(left_factor, right_factor):
    return jnp.einsum("heq,eqx->hex", left_factor, right_factor, preferred_element_type=jnp.float32)


def complex_apply(rounded, factors):
    real_part = contract(rounded[0], factors[0]) - contract(rounded[1], factors[1])
    imag_part = contract(rounded[0], factors[1]) + contract(rounded[1], factors[0])
    return jnp.stack([real_part, imag_part])


def apply_levels(state, own_factors, cross_factors, pattern, leaf_bits):
    for level in range(own_factors.shape[0]):
        pair_bit = leaf_bits - 1 - level % leaf_bits
        rounded = state.astype(jnp.bfloat16)
        self_term = complex_apply(rounded, own_factors[level])
        cross_term = complex_apply(rounded, cross_factors[level])
        incoming = from_partner(cross_term, "leaf", pair_bit)
        weight_matrix = pattern[level].astype(jnp.float32)[None, None, :, None]
        state = self_term + weight_matrix * incoming
    return state


def general(coeffs, own_factors, cross_factors, pattern, order):
    leaf_bits = lax.axis_size("leaf").bit_length() - 1
    local_blocks = coeffs.shape[2]
    state = apply_levels(coeffs, own_factors, cross_factors, pattern, leaf_bits)
    selected_rows = jnp.take(state, order, axis=3)
    flat = selected_rows.reshape(2, selected_rows.shape[1], local_blocks * selected_rows.shape[3], 1)
    return lax.all_to_all(flat, "leaf", split_axis=2, concat_axis=3, tiled=True)


def local(coeffs, own_factors, cross_factors, pattern, order):
    n, blocks = lax.axis_size("leaf"), coeffs.shape[2]
    if n == 2 * blocks and n <= 8 and own_factors.shape[0] == 6:
        return fused(coeffs, own_factors, cross_factors, pattern, order)
    return general(coeffs, own_factors, cross_factors, pattern, order)


def solution(mesh):
    in_specs = (
        P(None, "rhs", "leaf", None),
        P(None, None, "leaf", None, None),
        P(None, None, "leaf", None, None),
        P(None, "leaf"),
        P(),
    )
    out_specs = P(None, "rhs", "leaf", None)
    return jax.shard_map(local, mesh=mesh, in_specs=in_specs, out_specs=out_specs, check_vma=False)
```

time: 23.8 us -> 20.8 us (0.87)
  local copies, waits for them, and re-layouts: 1.57 us -> 0 us
  Pallas kernels: 22.1 us -> 20.6 us
    unnamed x1 -> x0, local copies, waits for them, and re-layouts: 1.57 us -> none
    pallas_call x1 -> x2, Pallas kernels: 22.1 us -> 20.6 us  [the longest x1 19.9 us: fused(): pl.pallas_call(functools.partial(window_kernel, n, levels, blocks, GROUPS...]
where the time goes in v2:
time: 20.8 us; the launch traced here: 20.6 us
  Pallas kernels  20.6 us (99%)
    pallas_call x1, Pallas kernels, fused(): pl.pallas_call(functools.partial(window_kernel, n, levels, blocks, GROUPS...  19.9 us
    pallas_call x1, Pallas kernels, fused(): pl.pallas_call(functools.partial(assemble_kernel, n, bits - 1 - (levels -...  0.74 us

profile of v2, /device:TPU:0, one launch (start us, length us, event | category | flops | bytes accessed | tf_op | source)
XLA Modules:
  0.0 20.6 jit_solution(597368684613984216)
XLA Ops:
  0.0 19.9 %shard_map.55.parts_ref = bf16[8,32,128]{2,1,0:T(8,128)(2,1)S(1)} custom-call(f32[128,128]{1,0:T(8,128)} %bitcast.6, bf16[6,2,4,128,128]{4,3,2,1,0:T(8,128)(2,1)} %own_hbm.1, bf16[6,2,4,128,128]{4,3,2,1,0:T(8,128)(2,1)} %cross_hbm.1, s32[4,6]{1,0:T(4,128)} %bitcast.7, s32[1,128]{1,0:T(1,128)} %bitcast.8), custom_call_target="tpu_custom_call" | custom-call | tf_op jit(solution)/shard_map/pallas_call | solution.py:208
  19.9 0.7 %shard_map.56 = f32[256,64]{1,0:T(8,128)} custom-call(bf16[8,32,128]{2,1,0:T(8,128)(2,1)S(1)} %shard_map.55.parts_ref), custom_call_target="tpu_custom_call" | custom-call | tf_op jit(solution)/shard_map/pallas_call | solution.py:232
